TPU v7x, 32 devices: a whole 2x2x4 slice. The times are simulated.
32 devices in a mesh: mem: 4 (over y, core), ctx: 8 (over z, x).
Axes of the slice: x: 2, y: 2, z: 4, core: 2. Of those that a mesh axis runs over, the one named last changes fastest.
Arguments:
- queries: bfloat16 [8, 512, 32, 128], P('ctx', 'mem'), may hold values from -6 to 6
- keys: bfloat16 [8, 512, 32, 128], P('ctx', 'mem'), may hold values from -6 to 6
- values: bfloat16 [8, 512, 32, 128], P('ctx', 'mem'), may hold values from -6 to 6
- log_decay: bfloat16 [8, 512, 32], P('ctx', 'mem'), may hold values from -1 to 0, as said below
- routes: int32 [8, 512, 2], P('ctx', 'mem'), may hold values from 0 to 3, all different within a row; in each aligned block of 128 rows (0 to 127, 128 to 255, ..., all dimensions but the last counted through in order) at most 72 rows name the same one
- route_weight: float32 [8, 512, 2], P('ctx', 'mem'), may hold values from 0.2 to 1
- gain: float32 [4096], replicated, may hold values from 0.25 to 1.75
Outputs:
- layer_out: bfloat16 [8, 512, 32, 128], P('ctx', 'mem')
Inputs may be any that keep to these rules, and one draw needn't show every extreme that they name: `routes`: A token's two memories differ. Among the tokens of one device (an aligned block of 128 tokens) no memory is named by more than 72 tokens, and in some such block a memory is named by exactly 72. `log_decay`: entries are negative.
All inputs are finite; a program needn't handle non-finite values.
Results may differ from a plain program's by a relative error of at most 0.015.
Values may be sent and summed in bfloat16 or wider, within the bound.
No kernel may reach another device: no remote copies, remote signals or barrier semaphores. Data moves between devices by JAX's collectives and lax.ppermute only.
A program may use at most 128 MiB of HBM per device.

v0:
```python
import math
import jax
import jax.numpy as jnp
from jax import lax
from jax.sharding import PartitionSpec as P


def as_sent(array):

    def short(part):
        return part.astype(jnp.bfloat16) if part.dtype == jnp.float32 else part

    return jax.tree.map(short, array)


def split_parts(matrix):
    high = matrix.astype(jnp.bfloat16)
    low = (matrix - high.astype(jnp.float32)).astype(jnp.bfloat16)
    return (high, low)


def head_norm(rows):
    square_mean = jnp.mean(rows * rows, axis=-1, keepdims=True)
    return rows * lax.rsqrt(square_mean + 1e-06)


def local_terms(keys_in, incoming_values, rates_in):
    running_decay = jnp.cumsum(rates_in.astype(jnp.float32), axis=0)
    total = running_decay[-1]
    retained_mask = jnp.exp(total[None, :] - running_decay)
    upper_scaled_state, lower_scaled_state = split_parts(
        keys_in.astype(jnp.float32) * retained_mask[:, :, None]
    )
    state_increment = jnp.einsum(
        "dyn,dye->yne", upper_scaled_state, incoming_values, preferred_element_type=jnp.float32
    )
    state_increment = state_increment + jnp.einsum(
        "dyn,dye->yne", lower_scaled_state, incoming_values, preferred_element_type=jnp.float32
    )
    return (running_decay, jnp.exp(total), state_increment)


def compose_rows(earlier, later):
    return (earlier[0] * later[0], later[0][..., None] * earlier[1] + later[1])


def incoming_state(decay_total, state_increment):
    heads = state_increment.shape[0]
    hdim = state_increment.shape[1]
    flat_rows = heads * hdim
    pieces = (
        lax.all_to_all(
            state_increment.reshape(1, flat_rows, hdim).astype(jnp.bfloat16),
            "ctx",
            split_axis=1,
            concat_axis=0,
            tiled=True,
        ).astype(jnp.float32),
        lax.all_to_all(
            jnp.repeat(decay_total, hdim).reshape(1, flat_rows).astype(jnp.bfloat16),
            "ctx",
            split_axis=1,
            concat_axis=0,
            tiled=True,
        ).astype(jnp.float32),
    )
    inclusive = lax.associative_scan(compose_rows, (pieces[1], pieces[0]), axis=0)
    shifted = jnp.concatenate([jnp.zeros_like(inclusive[1][:1]), inclusive[1][:-1]], axis=0)
    returned = lax.all_to_all(
        as_sent(shifted), "ctx", split_axis=0, concat_axis=1, tiled=True
    ).astype(shifted.dtype)
    return returned.reshape(heads, hdim, hdim)


def memory_readout(
    queries_in, keys_in, incoming_values, running_decay, entering_state, query_scale
):
    count_rows = queries_in.shape[0]
    heads = queries_in.shape[1]
    hdim = queries_in.shape[2]
    width = math.gcd(heads, 8)
    causal = jnp.arange(count_rows)[:, None] >= jnp.arange(count_rows)[None, :]

    def one_group(index, result):
        start = index * width
        query_group_rows = lax.dynamic_slice_in_dim(queries_in, start, width, 1)
        group_key = lax.dynamic_slice_in_dim(keys_in, start, width, 1)
        group_value = lax.dynamic_slice_in_dim(incoming_values, start, width, 1)
        group_cumul = lax.dynamic_slice_in_dim(running_decay, start, width, 1)
        group_state = lax.dynamic_slice_in_dim(entering_state, start, width, 0)
        head_cumul = group_cumul.T
        masked = jnp.where(causal, head_cumul[:, :, None] - head_cumul[:, None, :], -jnp.inf)
        scores = jnp.einsum(
            "ihd,jhd->hij", query_group_rows, group_key, preferred_element_type=jnp.float32
        )
        weights = (jnp.exp(masked) * scores * query_scale).astype(jnp.bfloat16)
        intra = jnp.einsum("hij,jhd->ihd", weights, group_value, preferred_element_type=jnp.float32)
        upper_state_part, lower_state_part = split_parts(group_state)
        across_block_output = jnp.einsum(
            "epm,pmx->epx", query_group_rows, upper_state_part, preferred_element_type=jnp.float32
        )
        across_block_output = across_block_output + jnp.einsum(
            "epm,pmx->epx", query_group_rows, lower_state_part, preferred_element_type=jnp.float32
        )
        across_block_output = across_block_output * (jnp.exp(group_cumul) * query_scale)[:, :, None]
        group_out = (intra + across_block_output).astype(jnp.bfloat16)
        return lax.dynamic_update_slice_in_dim(result, group_out, start, 1)

    return lax.fori_loop(
        0, heads // width, one_group, jnp.zeros((count_rows, heads, hdim), jnp.bfloat16)
    )


def shards(queries, keys, values, log_decay, routes, route_weight, gain):
    tokens_here = queries.shape[1]
    heads = queries.shape[2]
    hdim = queries.shape[3]
    memories = lax.axis_size("mem")
    capacity = 2 * tokens_here // memories + tokens_here // 16
    query_scale = hdim ** (-0.5)
    local_routes = routes[0]
    member = jnp.any(
        local_routes[:, :, None] == jnp.arange(memories, dtype=jnp.int32)[None, None, :], axis=1
    )
    counted = member.astype(jnp.int32)
    rank = jnp.cumsum(counted, axis=0) - counted
    match = member[None, :, :] & (
        rank[None, :, :] == jnp.arange(capacity, dtype=jnp.int32)[:, None, None]
    )
    source = jnp.sum(
        jnp.where(match, jnp.arange(tokens_here, dtype=jnp.int32)[None, :, None], 0), axis=1
    ).T.reshape(-1)
    filled = jnp.any(match, axis=1).T.reshape(-1)

    def packed(table):
        shaped = filled.reshape((-1,) + (1,) * (table.ndim - 1))
        rows_out = jnp.where(shaped, table[source], jnp.zeros((), table.dtype))
        return rows_out.reshape((memories, capacity) + table.shape[1:])

    query_send = packed(queries[0])
    key_send = packed(keys[0])
    value_send = packed(values[0])
    rate_send = packed(log_decay[0])
    count_rows = memories * capacity
    query_got, key_got, value_got, rate_got = (
        lax.all_to_all(query_send, "mem", split_axis=0, concat_axis=0, tiled=True),
        lax.all_to_all(key_send, "mem", split_axis=0, concat_axis=0, tiled=True),
        lax.all_to_all(value_send, "mem", split_axis=0, concat_axis=0, tiled=True),
        lax.all_to_all(rate_send, "mem", split_axis=0, concat_axis=0, tiled=True),
    )
    running_decay, decay_total, state_increment = local_terms(
        key_got.reshape(count_rows, heads, hdim),
        value_got.reshape(count_rows, heads, hdim),
        rate_got.reshape(count_rows, heads),
    )
    entering_state = incoming_state(decay_total, state_increment)
    readout = memory_readout(
        query_got.reshape(count_rows, heads, hdim),
        key_got.reshape(count_rows, heads, hdim),
        value_got.reshape(count_rows, heads, hdim),
        running_decay,
        entering_state,
        query_scale,
    )
    returned = lax.all_to_all(
        readout.reshape(memories, capacity, heads, hdim),
        "mem",
        split_axis=0,
        concat_axis=0,
        tiled=True,
    )
    flat = returned.reshape(count_rows, heads, hdim)
    picked_rank = jnp.take_along_axis(rank, local_routes, axis=1)
    slot_index = local_routes * capacity + picked_rank
    first_out = head_norm(flat[slot_index[:, 0]].astype(jnp.float32))
    second_out = head_norm(flat[slot_index[:, 1]].astype(jnp.float32))
    local_weight = route_weight[0]
    mixed = first_out * local_weight[:, 0, None, None] + second_out * local_weight[:, 1, None, None]
    return (mixed * gain.reshape(heads, hdim)).astype(jnp.bfloat16)[None]


def solution(mesh):
    return jax.shard_map(
        shards,
        mesh=mesh,
        in_specs=(
            P("ctx", "mem", None, None),
            P("ctx", "mem", None, None),
            P("ctx", "mem", None, None),
            P("ctx", "mem", None),
            P("ctx", "mem", None),
            P("ctx", "mem", None),
            P(),
        ),
        out_specs=P("ctx", "mem", None, None),
        check_vma=False,
    )
```

profile of v0, /device:TPU:0, one launch (start us, length us, event | category | flops | bytes accessed | tf_op | source)
XLA Modules:
  0.0 320.1 jit_solution(15708882655729172114)
XLA Ops:
  2.6 1.4 gather_fusion.1
  4.7 4.3 %all-to-all-start.1 = ((bf16[4,72,32]{1,2,0:T(8,128)(2,1)}), bf16[4,72,32]{1,2,0:T(8,128)(2,1)}, u32[]{:S(2)}, u32[]{:S(2)}) async-start(bf16[4,72,32]{1,2,0:T(8,128)(2,1)} %broadcast_select_fusion.3), calls=%async_computation.1 | async-start | bytes 65536 | tf_op jit(solution)/shard_map/all_to_all | solution.py:149
  9.0 2.3 gather_fusion.3
  11.3 3.7 %gather_fusion.2 = bf16[288,32,128]{2,1,0:T(8,128)(2,1)} fusion(bf16[128,32,128]{2,1,0:T(8,128)(2,1)} %bitcast.123, s32[1024]{0:T(1024)S(1)} %pad_clamp_fusion.2), kind=kCustom, calls=%fused_computation.2 | custom fusion | bytes 4719744 | tf_op jit(solution)/shard_map/gather | solution.py:137
  15.0 3.0 gather_fusion
  18.0 4.1 %broadcast_select_fusion = (bf16[4,72,32,128]{3,2,1,0:T(8,128)(2,1)S(1)}, bf16[4,72,32,128]{3,2,1,0:T(8,128)(2,1)}, bf16[4,72,32,128]{3,2,1,0:T(8,128)(2,1)}) fusion(bf16[4,72,32,128]{3,2,1,0:T(8,128)(2,1)S(1)} %bitcast.117, pred[4,72]{1,0:T(4,128)(4,1)S(1)} %bitcast.141, bf16[4,72,32,128]{3,2,1,0:T(8,128)(2,1)} %bitcast.118, ...), kind=kLoop, calls=%fused_computation.45 | loop fusion | flops 3538944 | bytes 14156064 | tf_op jit(solution)/shard_map/jit(_where)/select_n | solution.py:137
  22.1 2.4 copy.91
  24.4 3.9 %all-to-all-start.3 = ((bf16[4,72,32,128]{3,1,2,0:T(8,128)(2,1)}), bf16[4,72,32,128]{3,1,2,0:T(8,128)(2,1)S(1)}, u32[]{:S(2)}, u32[]{:S(2)}) async-start(bf16[4,72,32,128]{3,1,2,0:T(8,128)(2,1)} %copy.91), calls=%async_computation.3 | async-start | bytes 4718592 | tf_op jit(solution)/shard_map/all_to_all | solution.py:147
  28.3 4.0 %copy.82 = bf16[4,72,32,128]{3,1,2,0:T(8,128)(2,1)} copy(bf16[4,72,32,128]{3,2,1,0:T(8,128)(2,1)} %get-tuple-element.207) | data formatting | bytes 4718592 | tf_op jit(solution)/shard_map/jit(_where)/select_n | solution.py:137
  32.3 24.5 %all-to-all-done.3 = bf16[4,72,32,128]{3,1,2,0:T(8,128)(2,1)S(1)} async-done(((bf16[4,72,32,128]{3,1,2,0:T(8,128)(2,1)}), bf16[4,72,32,128]{3,1,2,0:T(8,128)(2,1)S(1)}, u32[]{:S(2)}, u32[]{:S(2)}) %all-to-all-start.3) | async-done | bytes 2359328 | tf_op jit(solution)/shard_map/all_to_all | solution.py:147
  56.8 4.5 %all-to-all-start = ((bf16[4,72,32,128]{3,1,2,0:T(8,128)(2,1)}), bf16[4,72,32,128]{3,1,2,0:T(8,128)(2,1)}, u32[]{:S(2)}, u32[]{:S(2)}) async-start(bf16[4,72,32,128]{3,1,2,0:T(8,128)(2,1)} %copy.82), calls=%async_computation | async-start | bytes 4718592 | tf_op jit(solution)/shard_map/all_to_all | solution.py:148
  66.6 1.8 copy.92
  68.4 4.5 %fusion.20 = (bf16[288,32,128]{2,1,0:T(8,128)(2,1)}, bf16[288,32,128]{2,1,0:T(8,128)(2,1)S(1)}) fusion(f32[288,32]{1,0:T(8,128)S(1)} %copy.93, bf16[4,72,32,128]{3,2,1,0:T(8,128)(2,1)} %copy.92), kind=kLoop, calls=%fused_computation.36 | loop fusion | flops 7077888 | bytes 7114752 | tf_op jit(solution)/shard_map/convert_element_type | solution.py:17
  72.8 17.0 %all-to-all-done = bf16[4,72,32,128]{3,1,2,0:T(8,128)(2,1)} async-done(((bf16[4,72,32,128]{3,1,2,0:T(8,128)(2,1)}), bf16[4,72,32,128]{3,1,2,0:T(8,128)(2,1)}, u32[]{:S(2)}, u32[]{:S(2)}) %all-to-all-start) | async-done | bytes 2359328 | tf_op jit(solution)/shard_map/all_to_all | solution.py:148
  89.9 6.6 %all-to-all-start.5 = ((bf16[8,2,256]{2,1,0:T(2,128)(2,1)}), bf16[8,2,256]{2,1,0:T(2,128)(2,1)S(1)}, u32[]{:S(2)}, u32[]{:S(2)}) async-start(bf16[8,2,256]{2,1,0:T(2,128)(2,1)} %reshape.334), calls=%async_computation.5 | async-start | bytes 16384 | tf_op jit(solution)/shard_map/all_to_all | solution.py:59
  96.5 1.9 copy.83
  98.3 2.2 fusion.21
  100.8 2.3 add_convert_fusion
  103.2 16.7 %copy.131 = bf16[1,4096,128]{2,0,1:T(2,128)(2,1)S(1)} copy(bf16[1,4096,128]{2,1,0:T(8,128)(2,1)S(1)} %bitcast.125) | data formatting | bytes 2097152 | tf_op jit(solution)/shard_map/convert_element_type | solution.py:53
  119.9 22.4 %reduce.12 = bf16[4096,128]{1,0:T(8,128)(2,1)S(1)} reduce(bf16[4096,1,128]{2,1,0:T(2,128)(2,1)S(1)} %bitcast.122, bf16[]{:T(256)} %broadcast.245), dimensions={1}, to_apply=%bitcast.100.reduce_sub_computation | reduce | bytes 2097154
  143.4 6.0 %all-to-all-start.4 = ((bf16[8,2,32768]{2,1,0:T(2,128)(2,1)}), bf16[8,2,32768]{2,1,0:T(2,128)(2,1)S(1)}, u32[]{:S(2)}, u32[]{:S(2)}) async-start(bf16[8,2,32768]{2,1,0:T(2,128)(2,1)} %reshape.332), calls=%async_computation.4 | async-start | bytes 2097152 | tf_op jit(solution)/shard_map/all_to_all | solution.py:52
  149.4 2.4 copy.89
  152.0 22.6 %all-to-all-done.4 = bf16[8,2,32768]{2,1,0:T(2,128)(2,1)S(1)} async-done(((bf16[8,2,32768]{2,1,0:T(2,128)(2,1)}), bf16[8,2,32768]{2,1,0:T(2,128)(2,1)S(1)}, u32[]{:S(2)}, u32[]{:S(2)}) %all-to-all-start.4) | async-done | bytes 1048608 | tf_op jit(solution)/shard_map/all_to_all | solution.py:52
  174.6 4.7 %all-to-all-start.2 = ((bf16[4,72,32,128]{3,1,2,0:T(8,128)(2,1)}), bf16[4,72,32,128]{3,1,2,0:T(8,128)(2,1)}, u32[]{:S(2)}, u32[]{:S(2)}) async-start(bf16[4,72,32,128]{3,1,2,0:T(8,128)(2,1)} %copy.89), calls=%async_computation.2 | async-start | bytes 4718592 | tf_op jit(solution)/shard_map/all_to_all | solution.py:146
  179.3 3.5 %reshape.333 = bf16[4096,1,128]{2,1,0:T(2,128)(2,1)} reshape(bf16[8,2,32768]{2,1,0:T(2,128)(2,1)S(1)} %all-to-all-done.4) | data formatting | bytes 2097152
  182.7 3.8 %bitcast_convert_fusion.1 = f32[1,4096,128]{2,0,1:T(1,128)S(1)} fusion(bf16[4096,1,128]{2,1,0:T(2,128)(2,1)} %reshape.333), kind=kLoop, calls=%fused_computation.114 | loop fusion | flops 524288 | bytes 3145728 | tf_op jit(solution)/shard_map/convert_element_type | solution.py:58
  186.5 1.9 slice.138
  190.7 1.1 pad.28
  191.8 1.8 pad_add_fusion
  193.6 2.7 pad.29
  196.3 2.4 add.166
  199.7 2.8 pad.43
  202.7 1.7 add_convert_fusion.1
  205.5 2.1 all-to-all-done.2
  207.6 3.6 %all-to-all-start.6 = ((bf16[8,512,128]{2,1,0:T(8,128)(2,1)}), bf16[8,512,128]{2,1,0:T(8,128)(2,1)S(1)}, u32[]{:S(2)}, u32[]{:S(2)}) async-start(bf16[8,512,128]{2,1,0:T(8,128)(2,1)} %concatenate.11), calls=%async_computation.6 | async-start | bytes 2097152 | tf_op jit(solution)/shard_map/all_to_all | solution.py:69
  211.2 3.6 %copy.90 = bf16[4,72,32,128]{3,2,1,0:T(8,128)(2,1)} copy(bf16[4,72,32,128]{3,1,2,0:T(8,128)(2,1)} %all-to-all-done.2) | data formatting | bytes 4718592 | tf_op jit(solution)/shard_map/all_to_all | solution.py:146
  214.7 22.1 %all-to-all-done.6 = bf16[8,512,128]{2,1,0:T(8,128)(2,1)S(1)} async-done(((bf16[8,512,128]{2,1,0:T(8,128)(2,1)}), bf16[8,512,128]{2,1,0:T(8,128)(2,1)S(1)}, u32[]{:S(2)}, u32[]{:S(2)}) %all-to-all-start.6) | async-done | bytes 1048608 | tf_op jit(solution)/shard_map/all_to_all | solution.py:69
  236.8 1.6 convert.19
  238.4 1.8 broadcast_in_dim.102
  240.2 33.5 %while.14 = (s32[]{:T(128)}, bf16[288,32,128]{2,0,1:T(8,128)(2,1)}, bf16[288,32,128]{2,0,1:T(8,128)(2,1)}, f32[288,32]{0,1:T(8,128)}, bf16[288,32,128]{2,1,0:T(8...) while((s32[]{:T(128)}, bf16[288,32,128]{2,0,1:T(8,128)(2,1)}, ...), condition=%wide.region_7.8_spmd.clone, body=%wide.region_6.7_spmd.clone.sunk | while | flops 495840512 | bytes 11659435 | solution.py:109
  240.9 1.3 constant_dynamic-slice_fusion.3
  242.3 2.6 convolution_bitcast_fusion.2
  244.8 1.3 fusion.65
  246.2 2.3 fusion.66
  249.2 1.3 constant_dynamic-slice_fusion.3
  250.6 2.6 convolution_bitcast_fusion.2
  253.2 1.3 fusion.65
  254.5 2.3 fusion.66
  257.6 1.3 constant_dynamic-slice_fusion.3
  258.9 2.6 convolution_bitcast_fusion.2
  261.5 1.3 fusion.65
  262.8 2.4 fusion.66
  266.0 1.3 constant_dynamic-slice_fusion.3
  267.3 2.6 convolution_bitcast_fusion.2
  269.9 1.3 fusion.65
  271.3 2.4 fusion.66
  273.7 4.0 %copy.102 = bf16[4,72,32,128]{3,2,1,0:T(8,128)(2,1)} copy(bf16[4,72,32,128]{3,1,0,2:T(8,128)(2,1)} %bitcast.116) | data formatting | bytes 4718592 | tf_op jit(solution)/shard_map/reshape | solution.py:166
  277.7 3.8 %all-to-all-start.7 = ((bf16[4,72,32,128]{3,2,1,0:T(8,128)(2,1)}), bf16[4,72,32,128]{3,2,1,0:T(8,128)(2,1)S(1)}, u32[]{:S(2)}, u32[]{:S(2)}) async-start(bf16[4,72,32,128]{3,2,1,0:T(8,128)(2,1)} %copy.102), calls=%async_computation.7 | async-start | bytes 4718592 | tf_op jit(solution)/shard_map/all_to_all | solution.py:165
  281.7 1.9 gather_fusion.6
  284.1 25.8 %all-to-all-done.7 = bf16[4,72,32,128]{3,2,1,0:T(8,128)(2,1)S(1)} async-done(((bf16[4,72,32,128]{3,2,1,0:T(8,128)(2,1)}), bf16[4,72,32,128]{3,2,1,0:T(8,128)(2,1)S(1)}, u32[]{:S(2)}, u32[]{:S(2)}) %all-to-all-start.7) | async-done | bytes 2359328 | tf_op jit(solution)/shard_map/all_to_all | solution.py:165
  309.9 1.4 copy-done.5
  311.3 2.4 gather_fusion.5
  313.7 2.4 gather_fusion.4
  317.5 2.7 fusion.29
  (104 shorter events, 19.4 us)
Async XLA Ops:
  0.0 9.0 %copy-start = (bf16[1,128,32,128]{3,2,1,0:T(8,128)(2,1)S(1)}, bf16[1,128,32,128]{3,2,1,0:T(8,128)(2,1)}, u32[]{:S(2)}) copy-start(bf16[1,128,32,128]{3,2,1,0:T(8,128)(2,1)} %param.10) | copy-start | bytes 3145732
  4.7 19.7 %all-to-all-start.1 = ((bf16[4,72,32]{1,2,0:T(8,128)(2,1)}), bf16[4,72,32]{1,2,0:T(8,128)(2,1)}, u32[]{:S(2)}, u32[]{:S(2)}) async-start(bf16[4,72,32]{1,2,0:T(8,128)(2,1)} %broadcast_select_fusion.3), calls=%async_computation.1 | async-start | bytes 65536 | tf_op jit(solution)/shard_map/all_to_all | solution.py:149
  11.3 3.7 %copy-start.7 = (bf16[1,128,32,128]{3,2,1,0:T(8,128)(2,1)S(1)}, bf16[1,128,32,128]{3,2,1,0:T(8,128)(2,1)}, u32[]{:S(2)}) copy-start(bf16[1,128,32,128]{3,2,1,0:T(8,128)(2,1)} %param.11) | copy-start | bytes 3145732
  24.4 32.4 %all-to-all-start.3 = ((bf16[4,72,32,128]{3,1,2,0:T(8,128)(2,1)}), bf16[4,72,32,128]{3,1,2,0:T(8,128)(2,1)S(1)}, u32[]{:S(2)}, u32[]{:S(2)}) async-start(bf16[4,72,32,128]{3,1,2,0:T(8,128)(2,1)} %copy.91), calls=%async_computation.3 | async-start | bytes 4718592 | tf_op jit(solution)/shard_map/all_to_all | solution.py:147
  56.8 33.0 %all-to-all-start = ((bf16[4,72,32,128]{3,1,2,0:T(8,128)(2,1)}), bf16[4,72,32,128]{3,1,2,0:T(8,128)(2,1)}, u32[]{:S(2)}, u32[]{:S(2)}) async-start(bf16[4,72,32,128]{3,1,2,0:T(8,128)(2,1)} %copy.82), calls=%async_computation | async-start | bytes 4718592 | tf_op jit(solution)/shard_map/all_to_all | solution.py:148
  89.9 53.6 %all-to-all-start.5 = ((bf16[8,2,256]{2,1,0:T(2,128)(2,1)}), bf16[8,2,256]{2,1,0:T(2,128)(2,1)S(1)}, u32[]{:S(2)}, u32[]{:S(2)}) async-start(bf16[8,2,256]{2,1,0:T(2,128)(2,1)} %reshape.334), calls=%async_computation.5 | async-start | bytes 16384 | tf_op jit(solution)/shard_map/all_to_all | solution.py:59
  98.3 2.2 copy-start.2
  98.3 2.5 copy-start.3
  142.3 7.1 %copy-start.4 = (bf16[4,72,32,128]{3,2,1,0:T(8,128)(2,1)S(1)}, bf16[4,72,32,128]{3,2,1,0:T(8,128)(2,1)}, u32[]{:S(2)}) copy-start(bf16[4,72,32,128]{3,2,1,0:T(8,128)(2,1)} %get-tuple-element.206) | copy-start | bytes 7077892
  143.4 31.1 %all-to-all-start.4 = ((bf16[8,2,32768]{2,1,0:T(2,128)(2,1)}), bf16[8,2,32768]{2,1,0:T(2,128)(2,1)S(1)}, u32[]{:S(2)}, u32[]{:S(2)}) async-start(bf16[8,2,32768]{2,1,0:T(2,128)(2,1)} %reshape.332), calls=%async_computation.4 | async-start | bytes 2097152 | tf_op jit(solution)/shard_map/all_to_all | solution.py:52
  174.6 33.0 %all-to-all-start.2 = ((bf16[4,72,32,128]{3,1,2,0:T(8,128)(2,1)}), bf16[4,72,32,128]{3,1,2,0:T(8,128)(2,1)}, u32[]{:S(2)}, u32[]{:S(2)}) async-start(bf16[4,72,32,128]{3,1,2,0:T(8,128)(2,1)} %copy.89), calls=%async_computation.2 | async-start | bytes 4718592 | tf_op jit(solution)/shard_map/all_to_all | solution.py:146
  189.1 0.7 copy-start.9
  196.3 2.4 copy-start.6
  198.7 1.0 copy-start.10
  199.6 2.9 copy-start.8
  207.6 29.2 %all-to-all-start.6 = ((bf16[8,512,128]{2,1,0:T(8,128)(2,1)}), bf16[8,512,128]{2,1,0:T(8,128)(2,1)S(1)}, u32[]{:S(2)}, u32[]{:S(2)}) async-start(bf16[8,512,128]{2,1,0:T(8,128)(2,1)} %concatenate.11), calls=%async_computation.6 | async-start | bytes 2097152 | tf_op jit(solution)/shard_map/all_to_all | solution.py:69
  277.7 3.8 %copy-start.12 = (s32[1,128,2]{1,2,0:T(2,128)S(1)}, s32[1,128,2]{1,2,0:T(2,128)}, u32[]{:S(2)}) copy-start(s32[1,128,2]{1,2,0:T(2,128)} %param.13) | copy-start | bytes 3076
  277.7 32.2 %all-to-all-start.7 = ((bf16[4,72,32,128]{3,2,1,0:T(8,128)(2,1)}), bf16[4,72,32,128]{3,2,1,0:T(8,128)(2,1)S(1)}, u32[]{:S(2)}, u32[]{:S(2)}) async-start(bf16[4,72,32,128]{3,2,1,0:T(8,128)(2,1)} %copy.102), calls=%async_computation.7 | async-start | bytes 4718592 | tf_op jit(solution)/shard_map/all_to_all | solution.py:165
  281.7 2.3 copy-start.13
  309.9 1.4 copy-start.5
  313.7 3.7 %copy-start.11 = (f32[4096]{0:T(1024)S(1)}, f32[4096]{0:T(1024)}, u32[]{:S(2)}) copy-start(f32[4096]{0:T(1024)} %param.15) | copy-start | bytes 49156
  316.2 4.0 %copy-start.1 = (bf16[1,128,32,128]{3,2,1,0:T(8,128)(2,1)S(1)}, bf16[1,128,32,128]{3,2,1,0:T(8,128)(2,1)}, u32[]{:S(2)}) copy-start(bf16[1,128,32,128]{3,2,1,0:T(8,128)(2,1)} %param.10) | copy-start | bytes 3145732
where the time goes:
time: 322 us; the launch traced here: 320 us
  waiting for transfers between devices  114 us (35%)
  local copies, waits for them, and re-layouts  83.6 us (26%)
  other arithmetic  55 us (17%)
  starting transfers between devices  37.3 us (12%)
  matrix products  29.6 us (9%)
    all_to_all x1, waiting for transfers between devices, shards(): lax.all_to_all(readout.reshape(memories, capacity, heads, hdim), 'mem', s...  25.8 us
    all_to_all x1, waiting for transfers between devices, shards(): lax.all_to_all(key_send, 'mem', split_axis=0, concat_axis=0, tiled=True)  24.5 us
    unnamed x2, other arithmetic  23.1 us
    all_to_all x1, waiting for transfers between devices, incoming_state(): lax.all_to_all(state_increment.reshape(1, flat_rows, hdim).astype(jnp.bfl...  22.6 us
    all_to_all x1, waiting for transfers between devices, incoming_state(): lax.all_to_all(as_sent(shifted), 'ctx', split_axis=0, concat_axis=1, tile...  22.1 us
    all_to_all x1, waiting for transfers between devices, shards(): lax.all_to_all(value_send, 'mem', split_axis=0, concat_axis=0, tiled=True)  17 us
    convert_element_type x1, local copies, waits for them, and re-layouts, incoming_state(): state_increment.reshape(1, flat_rows, hdim).astype(jnp.bfloat16)  16.7 us
    unnamed x37, local copies, waits for them, and re-layouts  10.6 us
  transfers between devices with their start and end apart: 8, of which 6 were waited for; matrix products, arithmetic and copies ran while one was open for 35% of the time, Pallas kernels for 0%

commit v1 on v0

--- a/solution.py
+++ b/solution.py
@@ -45,17 +45,22 @@
 
 
 def incoming_state(decay_total, state_increment):
+
+    def fill_the_block(buf):
+        return jnp.concatenate(
+            lax.all_to_all(
+                jnp.stack(jnp.split(buf, lax.axis_size("ctx"), axis=1), axis=0), "ctx", 0, 0
+            ),
+            axis=0,
+        )
+
     heads = state_increment.shape[0]
     hdim = state_increment.shape[1]
     flat_rows = heads * hdim
     pieces = (
-        lax.all_to_all(
-            state_increment.reshape(1, flat_rows, hdim).astype(jnp.bfloat16),
-            "ctx",
-            split_axis=1,
-            concat_axis=0,
-            tiled=True,
-        ).astype(jnp.float32),
+        fill_the_block(state_increment.reshape(1, flat_rows, hdim).astype(jnp.bfloat16)).astype(
+            jnp.float32
+        ),
         lax.all_to_all(
             jnp.repeat(decay_total, hdim).reshape(1, flat_rows).astype(jnp.bfloat16),
             "ctx",

time: 322 us -> 287 us (0.89)
  other arithmetic: 55 us -> 30.5 us
  local copies, waits for them, and re-layouts: 83.6 us -> 66 us
  waiting for transfers between devices: 114 us -> 122 us
    unnamed x2 -> x1, other arithmetic: 23.1 us -> 0.69 us
    convert_element_type x1 -> x0, local copies, waits for them, and re-layouts: 16.7 us -> none  [incoming_state(): state_increment.reshape(1, flat_rows, hdim).astype(jnp.bfloat16)]
    all_to_all x1, waiting for transfers between devices: 2.13 us -> 9.47 us  [shards(): lax.all_to_all(query_send, 'mem', split_axis=0, concat_axis=0, tiled=True)]
    unnamed x37 -> x40, local copies, waits for them, and re-layouts: 10.6 us -> 9.98 us
  transfers between devices with their start and end apart: 8 -> 8, of which waited for: 6 -> 6; matrix products, arithmetic and copies ran while one was open for 35% -> 24% of each run, Pallas kernels for 0% -> 0%
where the time goes in v1:
time: 287 us; the launch traced here: 285 us
  waiting for transfers between devices  122 us (43%)
  local copies, waits for them, and re-layouts  66 us (23%)
  starting transfers between devices  37 us (13%)
  other arithmetic  30.5 us (11%)
  matrix products  29.6 us (10%)
    all_to_all x1, waiting for transfers between devices, shards(): lax.all_to_all(readout.reshape(memories, capacity, heads, hdim), 'mem', s...  25.8 us
    all_to_all x1, waiting for transfers between devices, shards(): lax.all_to_all(key_send, 'mem', split_axis=0, concat_axis=0, tiled=True)  24.5 us
    all_to_all x1, waiting for transfers between devices, fill_the_block(): lax.all_to_all(jnp.stack(jnp.split(buf, lax.axis_size('ctx'), axis=1), ax...  22.6 us
    all_to_all x1, waiting for transfers between devices, incoming_state(): lax.all_to_all(as_sent(shifted), 'ctx', split_axis=0, concat_axis=1, tile...  22.1 us
    all_to_all x1, waiting for transfers between devices, shards(): lax.all_to_all(value_send, 'mem', split_axis=0, concat_axis=0, tiled=True)  17 us
    gather x5, local copies, waits for them, and re-layouts, packed(): rows_out = jnp.where(shaped, table[source], jnp.zeros((), table.dtype))  10.4 us
    dot_general x4, matrix products, one_group(): jnp.einsum('hij,jhd->ihd', weights, group_value, preferred_element_type=j...  10.3 us
    unnamed x40, local copies, waits for them, and re-layouts  9.98 us
  transfers between devices with their start and end apart: 8, of which 6 were waited for; matrix products, arithmetic and copies ran while one was open for 24% of the time, Pallas kernels for 0%

profile of v1, /device:TPU:0, one launch (start us, length us, event | category | flops | bytes accessed | tf_op | source)
XLA Modules:
  0.0 285.2 jit_solution(17300565901519007638)
XLA Ops:
  0.0 0.9 copy.73
  2.6 1.4 gather_fusion.1
  4.7 4.3 %all-to-all-start.1 = ((bf16[4,72,32]{1,2,0:T(8,128)(2,1)}), bf16[4,72,32]{1,2,0:T(8,128)(2,1)}, u32[]{:S(2)}, u32[]{:S(2)}) async-start(bf16[4,72,32]{1,2,0:T(8,128)(2,1)} %broadcast_select_fusion.3), calls=%async_computation.1 | async-start | bytes 65536 | tf_op jit(solution)/shard_map/all_to_all | solution.py:154
  9.0 2.3 gather_fusion.3
  11.3 3.7 %gather_fusion.2 = bf16[288,32,128]{2,1,0:T(8,128)(2,1)} fusion(bf16[128,32,128]{2,1,0:T(8,128)(2,1)} %bitcast.148, s32[1024]{0:T(1024)S(1)} %pad_clamp_fusion.2), kind=kCustom, calls=%fused_computation.2 | custom fusion | bytes 4719744 | tf_op jit(solution)/shard_map/gather | solution.py:142
  15.0 3.0 %gather_fusion = bf16[288,32,128]{2,1,0:T(8,128)(2,1)} fusion(bf16[128,32,128]{2,1,0:T(8,128)(2,1)S(1)} %bitcast.149, s32[1024]{0:T(1024)S(1)} %pad_clamp_fusion.2), kind=kCustom, calls=%fused_computation | custom fusion | bytes 4719744 | tf_op jit(solution)/shard_map/gather | solution.py:142
  18.0 4.1 %broadcast_select_fusion = (bf16[4,72,32,128]{3,2,1,0:T(8,128)(2,1)S(1)}, bf16[4,72,32,128]{3,2,1,0:T(8,128)(2,1)}, bf16[4,72,32,128]{3,2,1,0:T(8,128)(2,1)}) fusion(bf16[4,72,32,128]{3,2,1,0:T(8,128)(2,1)S(1)} %bitcast.143, pred[4,72]{1,0:T(4,128)(4,1)S(1)} %bitcast.172, bf16[4,72,32,128]{3,2,1,0:T(8,128)(2,1)} %bitcast.144, ...), kind=kLoop, calls=%fused_computation.45 | loop fusion | flops 3538944 | bytes 14156064 | tf_op jit(solution)/shard_map/jit(_where)/select_n | solution.py:142
  22.1 2.4 copy.87
  24.4 3.9 %all-to-all-start.3 = ((bf16[4,72,32,128]{3,1,2,0:T(8,128)(2,1)}), bf16[4,72,32,128]{3,1,2,0:T(8,128)(2,1)S(1)}, u32[]{:S(2)}, u32[]{:S(2)}) async-start(bf16[4,72,32,128]{3,1,2,0:T(8,128)(2,1)} %copy.87), calls=%async_computation.3 | async-start | bytes 4718592 | tf_op jit(solution)/shard_map/all_to_all | solution.py:152
  28.3 4.0 %copy.78 = bf16[4,72,32,128]{3,1,2,0:T(8,128)(2,1)} copy(bf16[4,72,32,128]{3,2,1,0:T(8,128)(2,1)} %get-tuple-element.209) | data formatting | bytes 4718592 | tf_op jit(solution)/shard_map/jit(_where)/select_n | solution.py:142
  32.3 24.5 %all-to-all-done.3 = bf16[4,72,32,128]{3,1,2,0:T(8,128)(2,1)S(1)} async-done(((bf16[4,72,32,128]{3,1,2,0:T(8,128)(2,1)}), bf16[4,72,32,128]{3,1,2,0:T(8,128)(2,1)S(1)}, u32[]{:S(2)}, u32[]{:S(2)}) %all-to-all-start.3) | async-done | bytes 2359328 | tf_op jit(solution)/shard_map/all_to_all | solution.py:152
  56.8 4.5 %all-to-all-start = ((bf16[4,72,32,128]{3,1,2,0:T(8,128)(2,1)}), bf16[4,72,32,128]{3,1,2,0:T(8,128)(2,1)}, u32[]{:S(2)}, u32[]{:S(2)}) async-start(bf16[4,72,32,128]{3,1,2,0:T(8,128)(2,1)} %copy.78), calls=%async_computation | async-start | bytes 4718592 | tf_op jit(solution)/shard_map/all_to_all | solution.py:153
  62.2 0.9 reduce-window.6
  66.6 1.8 copy.88
  68.4 4.5 %fusion.20 = (bf16[288,32,128]{2,1,0:T(8,128)(2,1)}, bf16[288,32,128]{2,1,0:T(8,128)(2,1)S(1)}) fusion(f32[288,32]{1,0:T(8,128)S(1)} %copy.89, bf16[4,72,32,128]{3,2,1,0:T(8,128)(2,1)} %copy.88), kind=kLoop, calls=%fused_computation.36 | loop fusion | flops 7077888 | bytes 7114752 | tf_op jit(solution)/shard_map/convert_element_type | solution.py:17
  72.8 17.0 %all-to-all-done = bf16[4,72,32,128]{3,1,2,0:T(8,128)(2,1)} async-done(((bf16[4,72,32,128]{3,1,2,0:T(8,128)(2,1)}), bf16[4,72,32,128]{3,1,2,0:T(8,128)(2,1)}, u32[]{:S(2)}, u32[]{:S(2)}) %all-to-all-start) | async-done | bytes 2359328 | tf_op jit(solution)/shard_map/all_to_all | solution.py:153
  89.9 6.6 %all-to-all-start.5 = ((bf16[8,2,256]{2,1,0:T(2,128)(2,1)}), bf16[8,2,256]{2,1,0:T(2,128)(2,1)S(1)}, u32[]{:S(2)}, u32[]{:S(2)}) async-start(bf16[8,2,256]{2,1,0:T(2,128)(2,1)} %reshape.330), calls=%async_computation.5 | async-start | bytes 16384 | tf_op jit(solution)/shard_map/all_to_all | solution.py:64
  96.5 1.9 copy.79
  98.3 2.2 fusion.21
  100.8 2.3 add_convert_fusion
  108.5 6.0 %all-to-all-start.4 = ((bf16[8,1,512,128]{3,2,1,0:T(8,128)(2,1)}), bf16[8,1,512,128]{3,2,1,0:T(8,128)(2,1)S(1)}, u32[]{:S(2)}, u32[]{:S(2)}) async-start(bf16[8,1,512,128]{3,2,1,0:T(8,128)(2,1)} %fusion.42), calls=%async_computation.4 | async-start | bytes 2097152 | tf_op jit(solution)/shard_map/all_to_all | solution.py:51
  114.5 2.4 copy.85
  117.0 22.6 %all-to-all-done.4 = bf16[8,1,512,128]{3,2,1,0:T(8,128)(2,1)S(1)} async-done(((bf16[8,1,512,128]{3,2,1,0:T(8,128)(2,1)}), bf16[8,1,512,128]{3,2,1,0:T(8,128)(2,1)S(1)}, u32[]{:S(2)}, u32[]{:S(2)}) %all-to-all-start.4) | async-done | bytes 1048608 | tf_op jit(solution)/shard_map/all_to_all | solution.py:51
  139.6 4.5 %all-to-all-start.2 = ((bf16[4,72,32,128]{3,1,2,0:T(8,128)(2,1)}), bf16[4,72,32,128]{3,1,2,0:T(8,128)(2,1)}, u32[]{:S(2)}, u32[]{:S(2)}) async-start(bf16[4,72,32,128]{3,1,2,0:T(8,128)(2,1)} %copy.85), calls=%async_computation.2 | async-start | bytes 4718592 | tf_op jit(solution)/shard_map/all_to_all | solution.py:151
  144.1 1.7 fusion.58
  148.0 1.1 pad.28
  149.2 1.8 pad_add_fusion
  151.0 2.7 pad.29
  153.7 2.4 add.166
  156.1 1.0 slice_bitcast_fusion
  157.4 2.8 pad.43
  160.4 1.7 add_convert_fusion.1
  162.1 1.0 concatenate.11
  163.2 9.5 %all-to-all-done.2 = bf16[4,72,32,128]{3,1,2,0:T(8,128)(2,1)} async-done(((bf16[4,72,32,128]{3,1,2,0:T(8,128)(2,1)}), bf16[4,72,32,128]{3,1,2,0:T(8,128)(2,1)}, u32[]{:S(2)}, u32[]{:S(2)}) %all-to-all-start.2) | async-done | bytes 2359328 | tf_op jit(solution)/shard_map/all_to_all | solution.py:151
  172.7 3.6 %all-to-all-start.6 = ((bf16[8,512,128]{2,1,0:T(8,128)(2,1)}), bf16[8,512,128]{2,1,0:T(8,128)(2,1)S(1)}, u32[]{:S(2)}, u32[]{:S(2)}) async-start(bf16[8,512,128]{2,1,0:T(8,128)(2,1)} %concatenate.11), calls=%async_computation.6 | async-start | bytes 2097152 | tf_op jit(solution)/shard_map/all_to_all | solution.py:74
  176.2 3.6 %copy.86 = bf16[4,72,32,128]{3,2,1,0:T(8,128)(2,1)} copy(bf16[4,72,32,128]{3,1,2,0:T(8,128)(2,1)} %all-to-all-done.2) | data formatting | bytes 4718592 | tf_op jit(solution)/shard_map/all_to_all | solution.py:151
  179.8 22.1 %all-to-all-done.6 = bf16[8,512,128]{2,1,0:T(8,128)(2,1)S(1)} async-done(((bf16[8,512,128]{2,1,0:T(8,128)(2,1)}), bf16[8,512,128]{2,1,0:T(8,128)(2,1)S(1)}, u32[]{:S(2)}, u32[]{:S(2)}) %all-to-all-start.6) | async-done | bytes 1048608 | tf_op jit(solution)/shard_map/all_to_all | solution.py:74
  201.9 1.6 convert.19
  203.4 1.8 broadcast_in_dim.102
  205.2 33.5 %while.14 = (s32[]{:T(128)}, bf16[288,32,128]{2,0,1:T(8,128)(2,1)}, bf16[288,32,128]{2,0,1:T(8,128)(2,1)}, f32[288,32]{0,1:T(8,128)}, bf16[288,32,128]{2,1,0:T(8...) while((s32[]{:T(128)}, bf16[288,32,128]{2,0,1:T(8,128)(2,1)}, ...), condition=%wide.region_7.8_spmd.clone, body=%wide.region_6.7_spmd.clone.sunk | while | flops 495840512 | bytes 11659435 | solution.py:114
  206.0 1.3 constant_dynamic-slice_fusion.3
  207.3 2.6 convolution_bitcast_fusion.2
  209.9 1.3 fusion.74
  211.2 2.3 fusion.75
  214.3 1.3 constant_dynamic-slice_fusion.3
  215.7 2.6 convolution_bitcast_fusion.2
  218.2 1.3 fusion.74
  219.6 2.3 fusion.75
  222.6 1.3 constant_dynamic-slice_fusion.3
  224.0 2.6 convolution_bitcast_fusion.2
  226.6 1.3 fusion.74
  227.9 2.4 fusion.75
  231.1 1.3 constant_dynamic-slice_fusion.3
  232.4 2.6 convolution_bitcast_fusion.2
  235.0 1.3 fusion.74
  236.3 2.4 fusion.75
  238.7 4.0 %copy.96 = bf16[4,72,32,128]{3,2,1,0:T(8,128)(2,1)} copy(bf16[4,72,32,128]{3,1,0,2:T(8,128)(2,1)} %bitcast.142) | data formatting | bytes 4718592 | tf_op jit(solution)/shard_map/reshape | solution.py:171
  242.7 3.8 %all-to-all-start.7 = ((bf16[4,72,32,128]{3,2,1,0:T(8,128)(2,1)}), bf16[4,72,32,128]{3,2,1,0:T(8,128)(2,1)S(1)}, u32[]{:S(2)}, u32[]{:S(2)}) async-start(bf16[4,72,32,128]{3,2,1,0:T(8,128)(2,1)} %copy.96), calls=%async_computation.7 | async-start | bytes 4718592 | tf_op jit(solution)/shard_map/all_to_all | solution.py:170
  246.8 1.9 gather_fusion.6
  249.1 25.8 %all-to-all-done.7 = bf16[4,72,32,128]{3,2,1,0:T(8,128)(2,1)S(1)} async-done(((bf16[4,72,32,128]{3,2,1,0:T(8,128)(2,1)}), bf16[4,72,32,128]{3,2,1,0:T(8,128)(2,1)S(1)}, u32[]{:S(2)}, u32[]{:S(2)}) %all-to-all-start.7) | async-done | bytes 2359328 | tf_op jit(solution)/shard_map/all_to_all | solution.py:170
  274.9 1.4 copy-done.5
  276.4 2.4 gather_fusion.5
  278.8 2.4 gather_fusion.4
  282.5 2.7 fusion.29
  (106 shorter events, 20.2 us)
Async XLA Ops:
  0.0 9.0 %copy-start = (bf16[1,128,32,128]{3,2,1,0:T(8,128)(2,1)S(1)}, bf16[1,128,32,128]{3,2,1,0:T(8,128)(2,1)}, u32[]{:S(2)}) copy-start(bf16[1,128,32,128]{3,2,1,0:T(8,128)(2,1)} %param.10) | copy-start | bytes 3145732
  4.7 19.7 %all-to-all-start.1 = ((bf16[4,72,32]{1,2,0:T(8,128)(2,1)}), bf16[4,72,32]{1,2,0:T(8,128)(2,1)}, u32[]{:S(2)}, u32[]{:S(2)}) async-start(bf16[4,72,32]{1,2,0:T(8,128)(2,1)} %broadcast_select_fusion.3), calls=%async_computation.1 | async-start | bytes 65536 | tf_op jit(solution)/shard_map/all_to_all | solution.py:154
  11.3 3.7 %copy-start.7 = (bf16[1,128,32,128]{3,2,1,0:T(8,128)(2,1)S(1)}, bf16[1,128,32,128]{3,2,1,0:T(8,128)(2,1)}, u32[]{:S(2)}) copy-start(bf16[1,128,32,128]{3,2,1,0:T(8,128)(2,1)} %param.11) | copy-start | bytes 3145732
  24.4 32.4 %all-to-all-start.3 = ((bf16[4,72,32,128]{3,1,2,0:T(8,128)(2,1)}), bf16[4,72,32,128]{3,1,2,0:T(8,128)(2,1)S(1)}, u32[]{:S(2)}, u32[]{:S(2)}) async-start(bf16[4,72,32,128]{3,1,2,0:T(8,128)(2,1)} %copy.87), calls=%async_computation.3 | async-start | bytes 4718592 | tf_op jit(solution)/shard_map/all_to_all | solution.py:152
  56.8 33.0 %all-to-all-start = ((bf16[4,72,32,128]{3,1,2,0:T(8,128)(2,1)}), bf16[4,72,32,128]{3,1,2,0:T(8,128)(2,1)}, u32[]{:S(2)}, u32[]{:S(2)}) async-start(bf16[4,72,32,128]{3,1,2,0:T(8,128)(2,1)} %copy.78), calls=%async_computation | async-start | bytes 4718592 | tf_op jit(solution)/shard_map/all_to_all | solution.py:153
  89.9 18.6 %all-to-all-start.5 = ((bf16[8,2,256]{2,1,0:T(2,128)(2,1)}), bf16[8,2,256]{2,1,0:T(2,128)(2,1)S(1)}, u32[]{:S(2)}, u32[]{:S(2)}) async-start(bf16[8,2,256]{2,1,0:T(2,128)(2,1)} %reshape.330), calls=%async_computation.5 | async-start | bytes 16384 | tf_op jit(solution)/shard_map/all_to_all | solution.py:64
  98.3 2.2 copy-start.2
  98.3 2.5 copy-start.3
  103.2 11.3 %copy-start.4 = (bf16[4,72,32,128]{3,2,1,0:T(8,128)(2,1)S(1)}, bf16[4,72,32,128]{3,2,1,0:T(8,128)(2,1)}, u32[]{:S(2)}) copy-start(bf16[4,72,32,128]{3,2,1,0:T(8,128)(2,1)} %get-tuple-element.208) | copy-start | bytes 7077892
  108.5 31.1 %all-to-all-start.4 = ((bf16[8,1,512,128]{3,2,1,0:T(8,128)(2,1)}), bf16[8,1,512,128]{3,2,1,0:T(8,128)(2,1)S(1)}, u32[]{:S(2)}, u32[]{:S(2)}) async-start(bf16[8,1,512,128]{3,2,1,0:T(8,128)(2,1)} %fusion.42), calls=%async_computation.4 | async-start | bytes 2097152 | tf_op jit(solution)/shard_map/all_to_all | solution.py:51
  139.6 33.0 %all-to-all-start.2 = ((bf16[4,72,32,128]{3,1,2,0:T(8,128)(2,1)}), bf16[4,72,32,128]{3,1,2,0:T(8,128)(2,1)}, u32[]{:S(2)}, u32[]{:S(2)}) async-start(bf16[4,72,32,128]{3,1,2,0:T(8,128)(2,1)} %copy.85), calls=%async_computation.2 | async-start | bytes 4718592 | tf_op jit(solution)/shard_map/all_to_all | solution.py:151
  146.5 0.7 copy-start.9
  153.7 3.4 %copy-start.6 = (f32[4,512,128]{2,1,0:T(8,128)S(1)}, f32[4,512,128]{2,1,0:T(8,128)}, u32[]{:S(2)}) copy-start(f32[4,512,128]{2,1,0:T(8,128)} %pad.29) | copy-start | bytes 3145732
  157.4 2.9 %copy-start.8 = (f32[4,512,128]{2,1,0:T(8,128)S(1)}, f32[4,512,128]{2,1,0:T(8,128)}, u32[]{:S(2)}) copy-start(f32[4,512,128]{2,1,0:T(8,128)} %add.166) | copy-start | bytes 3145732
  172.7 29.2 %all-to-all-start.6 = ((bf16[8,512,128]{2,1,0:T(8,128)(2,1)}), bf16[8,512,128]{2,1,0:T(8,128)(2,1)S(1)}, u32[]{:S(2)}, u32[]{:S(2)}) async-start(bf16[8,512,128]{2,1,0:T(8,128)(2,1)} %concatenate.11), calls=%async_computation.6 | async-start | bytes 2097152 | tf_op jit(solution)/shard_map/all_to_all | solution.py:74
  242.7 3.8 %copy-start.11 = (s32[1,128,2]{1,2,0:T(2,128)S(1)}, s32[1,128,2]{1,2,0:T(2,128)}, u32[]{:S(2)}) copy-start(s32[1,128,2]{1,2,0:T(2,128)} %param.13) | copy-start | bytes 3076
  242.7 32.2 %all-to-all-start.7 = ((bf16[4,72,32,128]{3,2,1,0:T(8,128)(2,1)}), bf16[4,72,32,128]{3,2,1,0:T(8,128)(2,1)S(1)}, u32[]{:S(2)}, u32[]{:S(2)}) async-start(bf16[4,72,32,128]{3,2,1,0:T(8,128)(2,1)} %copy.96), calls=%async_computation.7 | async-start | bytes 4718592 | tf_op jit(solution)/shard_map/all_to_all | solution.py:170
  246.8 2.3 copy-start.12
  274.9 1.4 copy-start.5
  278.8 3.7 %copy-start.10 = (f32[4096]{0:T(1024)S(1)}, f32[4096]{0:T(1024)}, u32[]{:S(2)}) copy-start(f32[4096]{0:T(1024)} %param.15) | copy-start | bytes 49156
  281.2 4.0 %copy-start.1 = (bf16[1,128,32,128]{3,2,1,0:T(8,128)(2,1)S(1)}, bf16[1,128,32,128]{3,2,1,0:T(8,128)(2,1)}, u32[]{:S(2)}) copy-start(bf16[1,128,32,128]{3,2,1,0:T(8,128)(2,1)} %param.10) | copy-start | bytes 3145732
